TPU v7x, 32 devices: a whole 2x2x4 slice. The times are simulated.
32 devices in a mesh: row: 8 (over z, y), col: 4 (over x, core).
Axes of the slice: x: 2, y: 2, z: 4, core: 2. Of those that a mesh axis runs over, the one named last changes fastest.
Arguments:
- star_state: float32 [7, 65536], P(None, ('row', 'col')), as said below
- active_index: int32 [8192], P(('row', 'col')), may hold values from 0 to 2047, as said below
- neighbour_index: int32 [8192, 128], P(('row', 'col')), may hold values from 0 to 2047, as said below
- assignment: int32 [8192, 1], P(('row', 'col')), may hold values from 0 to 31, as said below
- start_state: float32 [6, 8192], P(None, ('row', 'col')), may hold values from -6 to 6
- old_derivs: float32 [6, 8192], P(None, ('row', 'col')), may hold values from -12 to 12
- step_size: float32 [8192], P(('row', 'col')), may hold values from 0.1 to 1
Outputs:
- corrected: float32 [6, 8192], P(None, ('row', 'col'))
- forces: float32 [12, 8192], P(None, ('row', 'col'))
Inputs may be any that keep to these rules, and one draw needn't show every extreme that they name: `star_state`: row 6 (masses) is positive. `active_index`: within each aligned block of 256 entries (the active stars of one device) the entries are distinct. `neighbour_index`: the 128 entries of each row are distinct. `assignment`: within the rows of one device (aligned blocks of 256 rows) no device number appears more than 16 times, and some appears exactly 16 times.
All inputs are finite; a program needn't handle non-finite values.
Results may differ from a plain program's by a relative error of at most 0.000028.
Values sent between devices are 32-bit elements; how exact they have to be, the bound alone decides.
A program may use at most 192 MiB of HBM per device.

v0:
```python
import math

import jax
import jax.numpy as jnp
from jax import lax
from jax.sharding import PartitionSpec as P

soft_sq = 0.01


def pair_terms(active_parts, other_parts):
    sep_x = other_parts[0] - active_parts[0]
    sep_y = other_parts[1] - active_parts[1]
    sep_z = other_parts[2] - active_parts[2]
    rel_x = other_parts[3] - active_parts[3]
    rel_y = other_parts[4] - active_parts[4]
    rel_z = other_parts[5] - active_parts[5]
    dist_sq = sep_x * sep_x + sep_y * sep_y + sep_z * sep_z + soft_sq
    inverse = 1.0 / dist_sq
    strength = other_parts[6] * inverse * jnp.sqrt(inverse)
    radial = 3.0 * (sep_x * rel_x + sep_y * rel_y + sep_z * rel_z) * inverse
    pieces = [
        strength * sep_x,
        strength * sep_y,
        strength * sep_z,
        strength * (rel_x - radial * sep_x),
        strength * (rel_y - radial * sep_y),
        strength * (rel_z - radial * sep_z),
    ]
    return jnp.stack([jnp.sum(term, axis=-1) for term in pieces])


def hermite(total, start_state, old_derivs, step_size):
    half_step = step_size * 0.5
    twelfth = step_size * step_size / 12.0
    old_acc, old_jerk = (old_derivs[:3], old_derivs[3:])
    new_acc, new_jerk = (total[:3], total[3:])
    old_pos, old_vel = (start_state[:3], start_state[3:])
    new_vel = old_vel + (old_acc + new_acc) * half_step + (old_jerk - new_jerk) * twelfth
    new_pos = old_pos + (old_vel + new_vel) * half_step + (old_acc - new_acc) * twelfth
    return jnp.concatenate([new_pos, new_vel])


def body(star_state, active_index, neighbour_index, assignment, start_state, old_derivs, step_size):
    actives = active_index.shape[0]
    stars_dev = star_state.shape[1]
    rows_count = lax.axis_size("row")
    own_state = jnp.take(star_state[:6], active_index, axis=1)
    column_state = lax.all_gather(own_state, "row", axis=1, tiled=True)
    rows_all = rows_count * actives
    block_len = math.gcd(rows_all, 256)
    block_count = rows_all // block_len
    blocks = column_state.reshape(6, block_count, block_len).transpose(1, 0, 2)

    def add_piece(star_piece):
        star_rows = [star_piece[component][None, :] for component in range(7)]

        def one_block(block_state):
            return pair_terms(
                [block_state[component][:, None] for component in range(6)], star_rows
            )

        return lax.map(one_block, blocks)

    partial_value = add_piece(lax.all_gather(star_state, "col", axis=1, tiled=True))
    partial_value = partial_value.transpose(1, 0, 2).reshape(6, rows_all)
    summed = lax.psum(partial_value, "row")
    total = lax.dynamic_slice_in_dim(summed, lax.axis_index("row") * actives, actives, 1)
    target = assignment[:, 0]
    active_cols = [own_state[component][:, None] for component in range(6)]
    every_star = lax.all_gather(star_state, ("row", "col"), axis=1, tiled=True)
    neighbour_global = target[:, None] * stars_dev + neighbour_index
    tile_data = jnp.take(every_star, neighbour_global, axis=1)
    irregular = pair_terms(active_cols, [tile_data[component] for component in range(7)])
    regular = total - irregular
    corrected = hermite(total, start_state, old_derivs, step_size)
    return (corrected, jnp.concatenate([regular, irregular]))


def solution(mesh):
    in_specs = (
        P(None, ("row", "col")),
        P(("row", "col")),
        P(("row", "col"), None),
        P(("row", "col"), None),
        P(None, ("row", "col")),
        P(None, ("row", "col")),
        P(("row", "col")),
    )
    out_specs = (P(None, ("row", "col")), P(None, ("row", "col")))
    return jax.shard_map(body, mesh=mesh, in_specs=in_specs, out_specs=out_specs, check_vma=False)
```

profile of v0, /device:TPU:25, one launch (start us, length us, event | category | flops | bytes accessed | tf_op | source)
XLA Modules:
  0.0 355.0 jit_solution(17557504246800867277)
XLA Ops:
  7.2 0.0 all-gather.2.cloned.1.call-start
  7.2 2.2 copy.24
  9.4 0.0 all-gather.2.cloned.1.call-update
  9.4 0.7 compare_and_fusion.1
  10.1 0.7 compare_select_fusion.1
  10.8 6.5 %all_gather.9 = f32[7,8192]{1,0:T(8,128)S(1)} all-gather(f32[7,2048]{1,0:T(8,128)} %param.9), channel_id=1, replica_groups=mesh['row'=8,'col'=4] {'col'}, dimensions={1}, use_global_device_ids=true | all-gather | bytes 286720 | tf_op jit(solution)/shard_map/all_gather | solution.py:65
  17.3 0.2 fusion.28
  17.5 1.2 copy.22
  18.7 0.7 gather_fusion
  19.4 0.1 select_bitcast_fusion.1
  19.5 31.5 %all_gather.10 = f32[6,2048]{0,1:T(8,128)S(1)} all-gather(f32[6,256]{0,1:T(8,128)S(1)} %select_bitcast_fusion.1), channel_id=1, replica_groups=mesh['row'=8,'col'=4] {'row'}, dimensions={1}, use_global_device_ids=true | all-gather | bytes 55296 | tf_op jit(solution)/shard_map/all_gather | solution.py:49
  51.0 0.3 copy.23
  51.3 0.0 copy-start.3
  51.3 0.0 copy-start.1
  51.3 0.0 copy-start.2
  51.3 0.0 copy-start.4
  51.3 0.0 copy-start
  51.3 119.1 %while.10 = (s32[]{:T(128)}, f32[8,6,256]{2,1,0:T(8,128)S(1)}, f32[1,8192]{1,0:T(1,128)S(1)}, f32[1,8192]{1,0:T(1,128)S(1)}, f32[8,6,256]{2,1,0:T(8,128)S(1)}, /...) while((s32[]{:T(128)}, f32[8,6,256]{2,1,0:T(8,128)S(1)}, ...), condition=%wide.region_7.8_spmd, body=%wide.region_0.7_spmd.sunk | while | flops 83884552 | bytes 282877 | solution.py:63
  51.4 14.8 %fusion.30 = (f32[256]{0:T(256)S(1)}, f32[256]{0:T(256)S(1)}, f32[256]{0:T(256)S(1)}, f32[256]{0:T(256)S(1)}, f32[256]{0:T(256)S(1)}, /*index=5*/f32[256]{0:T(256)S(1)}) fusion(f32[256]{0:T(256)S(1)} %bitcast.170, f32[8192]{0:T(1024)S(1)} %bitcast.152, f32[256]{0:T(256)S(1)} %bitcast.167, f32[8192]{0:T(1024)S(1)} %bitcast.155, f32[256]{0:T(256)S(1)} %bitcast.168, ...), kind=kLoop, calls=%fused_computation.22.clone.1 | loop fusion | flops 83884544 | bytes 241664 | tf_op jit(solution)/shard_map/while/body/eval_jaxpr/reduce_sum | solution.py:30
  66.3 14.8 %fusion.30 = (f32[256]{0:T(256)S(1)}, f32[256]{0:T(256)S(1)}, f32[256]{0:T(256)S(1)}, f32[256]{0:T(256)S(1)}, f32[256]{0:T(256)S(1)}, /*index=5*/f32[256]{0:T(256)S(1)}) fusion(f32[256]{0:T(256)S(1)} %bitcast.170, f32[8192]{0:T(1024)S(1)} %bitcast.152, f32[256]{0:T(256)S(1)} %bitcast.167, f32[8192]{0:T(1024)S(1)} %bitcast.155, f32[256]{0:T(256)S(1)} %bitcast.168, ...), kind=kLoop, calls=%fused_computation.22.clone.1 | loop fusion | flops 83884544 | bytes 241664 | tf_op jit(solution)/shard_map/while/body/eval_jaxpr/reduce_sum | solution.py:30
  81.2 14.8 %fusion.30 = (f32[256]{0:T(256)S(1)}, f32[256]{0:T(256)S(1)}, f32[256]{0:T(256)S(1)}, f32[256]{0:T(256)S(1)}, f32[256]{0:T(256)S(1)}, /*index=5*/f32[256]{0:T(256)S(1)}) fusion(f32[256]{0:T(256)S(1)} %bitcast.170, f32[8192]{0:T(1024)S(1)} %bitcast.152, f32[256]{0:T(256)S(1)} %bitcast.167, f32[8192]{0:T(1024)S(1)} %bitcast.155, f32[256]{0:T(256)S(1)} %bitcast.168, ...), kind=kLoop, calls=%fused_computation.22.clone.1 | loop fusion | flops 83884544 | bytes 241664 | tf_op jit(solution)/shard_map/while/body/eval_jaxpr/reduce_sum | solution.py:30
  96.0 14.8 %fusion.30 = (f32[256]{0:T(256)S(1)}, f32[256]{0:T(256)S(1)}, f32[256]{0:T(256)S(1)}, f32[256]{0:T(256)S(1)}, f32[256]{0:T(256)S(1)}, /*index=5*/f32[256]{0:T(256)S(1)}) fusion(f32[256]{0:T(256)S(1)} %bitcast.170, f32[8192]{0:T(1024)S(1)} %bitcast.152, f32[256]{0:T(256)S(1)} %bitcast.167, f32[8192]{0:T(1024)S(1)} %bitcast.155, f32[256]{0:T(256)S(1)} %bitcast.168, ...), kind=kLoop, calls=%fused_computation.22.clone.1 | loop fusion | flops 83884544 | bytes 241664 | tf_op jit(solution)/shard_map/while/body/eval_jaxpr/reduce_sum | solution.py:30
  110.9 14.8 %fusion.30 = (f32[256]{0:T(256)S(1)}, f32[256]{0:T(256)S(1)}, f32[256]{0:T(256)S(1)}, f32[256]{0:T(256)S(1)}, f32[256]{0:T(256)S(1)}, /*index=5*/f32[256]{0:T(256)S(1)}) fusion(f32[256]{0:T(256)S(1)} %bitcast.170, f32[8192]{0:T(1024)S(1)} %bitcast.152, f32[256]{0:T(256)S(1)} %bitcast.167, f32[8192]{0:T(1024)S(1)} %bitcast.155, f32[256]{0:T(256)S(1)} %bitcast.168, ...), kind=kLoop, calls=%fused_computation.22.clone.1 | loop fusion | flops 83884544 | bytes 241664 | tf_op jit(solution)/shard_map/while/body/eval_jaxpr/reduce_sum | solution.py:30
  125.8 14.8 %fusion.30 = (f32[256]{0:T(256)S(1)}, f32[256]{0:T(256)S(1)}, f32[256]{0:T(256)S(1)}, f32[256]{0:T(256)S(1)}, f32[256]{0:T(256)S(1)}, /*index=5*/f32[256]{0:T(256)S(1)}) fusion(f32[256]{0:T(256)S(1)} %bitcast.170, f32[8192]{0:T(1024)S(1)} %bitcast.152, f32[256]{0:T(256)S(1)} %bitcast.167, f32[8192]{0:T(1024)S(1)} %bitcast.155, f32[256]{0:T(256)S(1)} %bitcast.168, ...), kind=kLoop, calls=%fused_computation.22.clone.1 | loop fusion | flops 83884544 | bytes 241664 | tf_op jit(solution)/shard_map/while/body/eval_jaxpr/reduce_sum | solution.py:30
  140.7 14.8 %fusion.30 = (f32[256]{0:T(256)S(1)}, f32[256]{0:T(256)S(1)}, f32[256]{0:T(256)S(1)}, f32[256]{0:T(256)S(1)}, f32[256]{0:T(256)S(1)}, /*index=5*/f32[256]{0:T(256)S(1)}) fusion(f32[256]{0:T(256)S(1)} %bitcast.170, f32[8192]{0:T(1024)S(1)} %bitcast.152, f32[256]{0:T(256)S(1)} %bitcast.167, f32[8192]{0:T(1024)S(1)} %bitcast.155, f32[256]{0:T(256)S(1)} %bitcast.168, ...), kind=kLoop, calls=%fused_computation.22.clone.1 | loop fusion | flops 83884544 | bytes 241664 | tf_op jit(solution)/shard_map/while/body/eval_jaxpr/reduce_sum | solution.py:30
  155.6 14.8 %fusion.30 = (f32[256]{0:T(256)S(1)}, f32[256]{0:T(256)S(1)}, f32[256]{0:T(256)S(1)}, f32[256]{0:T(256)S(1)}, f32[256]{0:T(256)S(1)}, /*index=5*/f32[256]{0:T(256)S(1)}) fusion(f32[256]{0:T(256)S(1)} %bitcast.170, f32[8192]{0:T(1024)S(1)} %bitcast.152, f32[256]{0:T(256)S(1)} %bitcast.167, f32[8192]{0:T(1024)S(1)} %bitcast.155, f32[256]{0:T(256)S(1)} %bitcast.168, ...), kind=kLoop, calls=%fused_computation.22.clone.1 | loop fusion | flops 83884544 | bytes 241664 | tf_op jit(solution)/shard_map/while/body/eval_jaxpr/reduce_sum | solution.py:30
  170.4 30.2 %psum.7 = f32[6,2048]{1,0:T(8,128)S(1)} all-reduce(f32[6,2048]{1,0:T(8,128)S(1)} %bitcast.151), channel_id=1, replica_groups=mesh['row'=8,'col'=4] {'row'}, use_global_device_ids=true, to_apply=%region_8.9 | all-reduce | flops 12288 | bytes 98304 | tf_op jit(solution)/shard_map/psum | solution.py:67
  200.6 0.0 copy-done.3
  200.6 0.0 copy-done.1
  200.7 0.0 copy-done.2
  200.7 0.1 multiply_add_fusion
  200.8 0.6 pad_maximum_fusion
  201.4 0.5 slice_reduce_fusion.2
  201.9 0.0 copy-done.4
  201.9 0.0 copy-done
  201.9 0.1 compare_and_fusion
  202.0 0.1 bitcast_clamp_fusion
  202.1 15.2 %all-gather.2.cloned.1.call-done = f32[7,65536]{0,1:T(8,128)} async-done(((f32[7,2048]{0,1:T(8,128)}), f32[7,65536]{0,1:T(8,128)}) %all-gather.2.cloned.1.call-update) | async-done | bytes 1835024 | tf_op jit(solution)/shard_map/all_gather | solution.py:71
  217.4 118.8 %gather_fusion.1 = f32[32768,7]{1,0:T(8,128)} fusion(f32[7,65536]{0,1:T(8,128)} %all-gather.2.cloned.1.call-done, s32[32768]{0:T(1024)S(1)} %bitcast_clamp_fusion), kind=kCustom, calls=%fused_computation.1 | custom fusion | bytes 1966080 | tf_op jit(solution)/shard_map/jit(_take)/gather | solution.py:73
  336.2 9.8 %copy.25 = f32[256,128,7]{1,0,2:T(8,128)S(1)} copy(f32[256,128,7]{2,1,0:T(8,128)} %bitcast.147) | data formatting | bytes 1835008 | tf_op jit(solution)/shard_map/jit(_take)/gather | solution.py:73
  346.0 0.1 select_bitcast_fusion
  346.0 0.3 multiply_multiply_fusion
  346.3 0.5 multiply_reduce_fusion
  346.9 1.2 concatenate.8
  (30 shorter events, 0.5 us)
Async XLA Ops:
  7.2 210.2 %all-gather.2.cloned.1.call-start = ((), (), s32[]{:S(2)}) async-start(), calls=%async_computation | async-start | bytes 34603008 | tf_op jit(solution)/shard_map/all_gather | solution.py:71
  51.3 149.3 %copy-start.3 = (f32[256]{0:T(256)S(1)}, f32[256]{0:T(256)}, u32[]{:S(2)}) copy-start(f32[256]{0:T(256)} %param.15) | copy-start | bytes 3076
  51.3 149.3 %copy-start.1 = (f32[6,256]{1,0:T(8,128)S(1)}, f32[6,256]{1,0:T(8,128)}, u32[]{:S(2)}) copy-start(f32[6,256]{1,0:T(8,128)} %param.13) | copy-start | bytes 18436
  51.3 149.3 %copy-start.2 = (f32[6,256]{1,0:T(8,128)S(1)}, f32[6,256]{1,0:T(8,128)}, u32[]{:S(2)}) copy-start(f32[6,256]{1,0:T(8,128)} %param.14) | copy-start | bytes 18436
  51.3 150.5 %copy-start.4 = (s32[256,1]{0,1:T(1,128)S(1)}, s32[256,1]{0,1:T(1,128)}, u32[]{:S(2)}) copy-start(s32[256,1]{0,1:T(1,128)} %param.12) | copy-start | bytes 3076
  51.3 150.5 %copy-start = (s32[256,128]{1,0:T(8,128)S(1)}, s32[256,128]{1,0:T(8,128)}, u32[]{:S(2)}) copy-start(s32[256,128]{1,0:T(8,128)} %param.11) | copy-start | bytes 393220
Sparse Core Ops, SparseCore 0:
  10.8 206.4 all-gather.1
where the time goes:
time: 358 us; the launch traced here: 355 us
  local copies, waits for them, and re-layouts  135 us (38%)
  other arithmetic  122 us (34%)
  blocking collectives  68.2 us (19%)
  waiting for transfers between devices  15.3 us (4%)
  between operations  14.2 us (4%)
    gather x2, local copies, waits for them, and re-layouts, body(): tile_data = jnp.take(every_star, neighbour_global, axis=1)  129 us
    reduce_sum x9, other arithmetic, pair_terms(): return jnp.stack([jnp.sum(term, axis=-1) for term in pieces])  119 us
    all_gather x1, blocking collectives, body(): column_state = lax.all_gather(own_state, 'row', axis=1, tiled=True)  31.5 us
    psum x1, blocking collectives, body(): summed = lax.psum(partial_value, 'row')  30.2 us
    all_gather x1, waiting for transfers between devices, body(): every_star = lax.all_gather(star_state, ('row', 'col'), axis=1, tiled=True)  15.2 us
  transfers between devices with their start and end apart: 1, of which 1 were waited for; matrix products, arithmetic and copies ran while one was open for 35% of the time, Pallas kernels for 0%

commit v1 on v0

v1 whole, which is shorter than its diff:
```python
import functools

import jax
import jax.numpy as jnp
from jax import lax
from jax.experimental import pallas as pl
from jax.experimental.pallas import tpu as pltpu
from jax.sharding import PartitionSpec as P

soft_sq = 0.01
LANES = 128
MESH = pl.DeviceIdType.MESH


def pair_sums(q, star, acc):
    dx, dy, dz = star[0] - q[0], star[1] - q[1], star[2] - q[2]
    ux, uy, uz = star[3] - q[3], star[4] - q[4], star[5] - q[5]
    s = dx * dx + dy * dy + dz * dz + soft_sq
    r = lax.rsqrt(s)
    inv = r * r
    w = (star[6] * r) * inv
    wk = w * ((dx * ux + dy * uy + dz * uz) * inv)
    return [
        acc[0] + w * dx,
        acc[1] + w * dy,
        acc[2] + w * dz,
        acc[3] + w * ux,
        acc[4] + w * uy,
        acc[5] + w * uz,
        acc[6] + wk * dx,
        acc[7] + wk * dy,
        acc[8] + wk * dz,
    ]


def lane_gather(load_tile, tiles, idx):
    low = idx % LANES
    high = idx // LANES
    out = jnp.zeros(idx.shape, jnp.float32)
    for t in range(tiles):
        got = jnp.take_along_axis(load_tile(t), low, axis=1)
        out = jnp.where(high == t, got, out)
    return out


def fill_states(star_ref, index_ref, q_ref):
    tiles = star_ref.shape[1] // LANES
    for part in range(index_ref.shape[1] // LANES):
        cols = slice(part * LANES, (part + 1) * LANES)
        idx = jnp.broadcast_to(index_ref[:, cols], (8, LANES))
        state = lane_gather(
            lambda t: star_ref[:, t * LANES : (t + 1) * LANES], tiles, idx
        )
        turned = jnp.transpose(state)
        for c in range(6):
            q_ref[c, cols, :] = jnp.broadcast_to(turned[:, c : c + 1], (LANES, LANES))


def rows_of(sums):
    actives = sums[0].shape[0]
    lane = lax.broadcasted_iota(jnp.int32, (actives, LANES), 1)
    wide = jnp.zeros((actives, LANES), jnp.float32)
    for c, col in enumerate(sums):
        wide = jnp.where(lane == c, jnp.broadcast_to(col, wide.shape), wide)
    return jnp.transpose(wide)[:8, :]


def total_kernel(axes, group, star_ref, index_ref, total_ref, slots, q_ref, acc_ref,
                 send_sem, recv_sem, own_sem):
    rows, cols = axes
    n = rows * cols
    me = lax.axis_index("row") * cols + lax.axis_index("col")
    actives = index_ref.shape[1]
    tiles = star_ref.shape[1] // LANES
    barrier = pltpu.get_barrier_semaphore()

    def place(k):
        other = lax.rem(me + k, n)
        return (lax.div(other, cols), lax.rem(other, cols))

    @pl.loop(1, n)
    def _(k):
        pl.semaphore_signal(barrier, inc=1, device_id=place(k), device_id_type=MESH)

    own = pltpu.make_async_copy(star_ref, slots.at[me], own_sem)
    own.start()
    fill_states(star_ref, index_ref, q_ref)
    acc_ref[...] = jnp.zeros_like(acc_ref)

    def add_block(block):
        @pl.loop(0, actives // (8 * group))
        def _(g):
            for sub in range(group):
                at = pl.ds(pl.multiple_of(g * (8 * group) + 8 * sub, 8), 8)
                q = [q_ref[c, at, :] for c in range(6)]
                acc = [acc_ref[c, at, :] for c in range(9)]
                for t in range(tiles):
                    lanes = slice(t * LANES, (t + 1) * LANES)
                    star = [jnp.broadcast_to(block[c : c + 1, lanes], (8, LANES)) for c in range(7)]
                    acc = pair_sums(q, star, acc)
                for c in range(9):
                    acc_ref[c, at, :] = acc[c]

    def copy(k):
        return pltpu.make_async_remote_copy(
            src_ref=star_ref, dst_ref=slots.at[me], send_sem=send_sem.at[k],
            recv_sem=recv_sem.at[k], device_id=place(k), device_id_type=MESH,
        )

    pl.semaphore_wait(barrier, n - 1)

    @pl.loop(1, n)
    def _(k):
        copy(k).start()

    add_block(star_ref)

    @pl.loop(1, n)
    def _(k):
        source = lax.rem(me + n - k, n)
        pltpu.make_async_remote_copy(
            src_ref=star_ref, dst_ref=slots.at[source], send_sem=send_sem.at[k],
            recv_sem=recv_sem.at[k], device_id=place(k), device_id_type=MESH,
        ).wait_recv()
        add_block(slots.at[source])

    @pl.loop(1, n)
    def _(k):
        copy(k).wait_send()

    own.wait()
    sums = [jnp.sum(acc_ref[c], axis=1, keepdims=True) for c in range(9)]
    jerk = [sums[3 + c] - 3.0 * sums[6 + c] for c in range(3)]
    total_ref[...] = rows_of(sums[:3] + jerk)


def finish_kernel(target_ref, every_ref, star_ref, index_ref, near_ref, total_ref, start_ref,
                  old_ref, step_ref, corrected_ref, forces_ref, q_ref, tile_ref, irr_ref):
    actives = index_ref.shape[1]
    tiles = star_ref.shape[1] // LANES
    fill_states(star_ref, index_ref, q_ref)

    @pl.loop(0, actives // 8)
    def _(g):
        base = pl.multiple_of(g * 8, 8)
        near = near_ref[pl.ds(base, 8), :]
        for i in range(8):
            block = every_ref.at[target_ref[base + i]]
            idx = jnp.broadcast_to(near[i : i + 1, :], (8, LANES))
            tile_ref[pl.ds(8 * i, 8), :] = lane_gather(
                lambda t: block[:, t * LANES : (t + 1) * LANES], tiles, idx
            )
        star = [tile_ref[pl.ds(c, 8, stride=8), :] for c in range(7)]
        q = [q_ref[c, pl.ds(base, 8), :] for c in range(6)]
        acc = pair_sums(q, star, [jnp.zeros((8, LANES), jnp.float32)] * 9)
        lane = lax.broadcasted_iota(jnp.int32, (8, LANES), 1)
        wide = jnp.zeros((8, LANES), jnp.float32)
        for c in range(3):
            wide = jnp.where(lane == c, jnp.sum(acc[c], axis=1, keepdims=True), wide)
            jerk = jnp.sum(acc[3 + c] - 3.0 * acc[6 + c], axis=1, keepdims=True)
            wide = jnp.where(lane == 3 + c, jerk, wide)
        irr_ref[pl.ds(base, 8), :] = wide

    irregular = jnp.transpose(irr_ref[...])[:6, :]
    total = total_ref[:6, :]
    forces_ref[0:6, :] = total - irregular
    forces_ref[6:12, :] = irregular
    h = step_ref[...]
    half = h * 0.5
    twelfth = h * h / 12.0
    a0, j0 = old_ref[0:3, :], old_ref[3:6, :]
    a1, j1 = total[0:3], total[3:6]
    x0, v0 = start_ref[0:3, :], start_ref[3:6, :]
    v1 = v0 + (a0 + a1) * half + (j0 - j1) * twelfth
    corrected_ref[0:3, :] = x0 + (v0 + v1) * half + (a0 - a1) * twelfth
    corrected_ref[3:6, :] = v1


def body(axes, star_state, active_index, neighbour_index, assignment, start_state, old_derivs, step_size):
    n = axes[0] * axes[1]
    stars = star_state.shape[1]
    actives = active_index.shape[0]
    vmem = pl.BlockSpec(memory_space=pltpu.VMEM)
    star8 = jnp.pad(star_state, ((0, 1), (0, 0)))
    index = active_index.reshape(1, actives)
    f32 = jnp.float32
    total, every = pl.pallas_call(
        functools.partial(total_kernel, axes, GROUP),
        out_shape=(jax.ShapeDtypeStruct((8, actives), f32), jax.ShapeDtypeStruct((n, 8, stars), f32)),
        in_specs=[vmem, vmem],
        out_specs=(vmem, vmem),
        scratch_shapes=[
            pltpu.VMEM((6, actives, LANES), f32),
            pltpu.VMEM((9, actives, LANES), f32),
            pltpu.SemaphoreType.DMA((n,)),
            pltpu.SemaphoreType.DMA((n,)),
            pltpu.SemaphoreType.DMA,
        ],
        compiler_params=pltpu.CompilerParams(collective_id=0, has_side_effects=True),
        name="total",
    )(star8, index)
    return pl.pallas_call(
        finish_kernel,
        out_shape=(jax.ShapeDtypeStruct((6, actives), f32), jax.ShapeDtypeStruct((12, actives), f32)),
        in_specs=[pl.BlockSpec(memory_space=pltpu.SMEM)] + [vmem] * 8,
        out_specs=(vmem, vmem),
        scratch_shapes=[
            pltpu.VMEM((6, actives, LANES), f32),
            pltpu.VMEM((64, LANES), f32),
            pltpu.VMEM((actives, LANES), f32),
        ],
        name="finish",
    )(assignment[:, 0], every, star8, index, neighbour_index, total, start_state, old_derivs,
      step_size.reshape(1, actives))


GROUP = 4


def solution(mesh):
    axes = (mesh.shape["row"], mesh.shape["col"])
    split = P(None, ("row", "col"))
    in_specs = (split, P(("row", "col")), P(("row", "col"), None), P(("row", "col"), None),
                split, split, P(("row", "col")))
    return jax.shard_map(functools.partial(body, axes), mesh=mesh, in_specs=in_specs,
                         out_specs=(split, split), check_vma=False)
```

time: 358 us -> 133 us (0.37)
  local copies, waits for them, and re-layouts: 135 us -> 1.48 us
  Pallas kernels: 0 us -> 131 us
  other arithmetic: 122 us -> 0 us
  blocking collectives: 68.2 us -> 0 us
  waiting for transfers between devices: 15.3 us -> 0 us
  between operations: 14.2 us -> 0.64 us
    pallas_call x0 -> x2, Pallas kernels: none -> 131 us  [the longest x1 115 us: body(): pl.pallas_call(functools.partial(total_kernel, axes, GROUP), out_shape=(j...]
    gather x3 -> x0, local copies, waits for them, and re-layouts: 129 us -> none  [the longest x2 129 us: body(): tile_data = jnp.take(every_star, neighbour_global, axis=1)]
    reduce_sum x9 -> x0, other arithmetic: 119 us -> none  [pair_terms(): return jnp.stack([jnp.sum(term, axis=-1) for term in pieces])]
    all_gather x2 -> x0, blocking collectives: 38 us -> none  [the longest x1 31.5 us: body(): column_state = lax.all_gather(own_state, 'row', axis=1, tiled=True)]
    psum x1 -> x0, blocking collectives: 30.2 us -> none  [body(): summed = lax.psum(partial_value, 'row')]
    all_gather x1 -> x0, waiting for transfers between devices: 15.2 us -> none  [body(): every_star = lax.all_gather(star_state, ('row', 'col'), axis=1, tiled=True)]
  transfers between devices with their start and end apart: 1 -> 0, of which waited for: 1 -> 0; matrix products, arithmetic and copies ran while one was open for 35% -> 0% of each run, Pallas kernels for 0% -> 0%
where the time goes in v1:
time: 133 us
  Pallas kernels  131 us (98%)
  local copies, waits for them, and re-layouts  1.48 us (1%)
    pallas_call x1, Pallas kernels, body(): pl.pallas_call(functools.partial(total_kernel, axes, GROUP), out_shape=(j...  115 us
    pallas_call x1, Pallas kernels, body(): pl.pallas_call(finish_kernel, out_shape=(jax.ShapeDtypeStruct((6, actives...  15.7 us

profile of v1, /device:TPU:25, one launch (start us, length us, event | category | flops | bytes accessed | tf_op | source)
XLA Modules:
  0.0 132.6 jit_solution(13051689488135810467)
XLA Ops:
  0.6 1.5 %pad.4.star_ref = f32[8,2048]{1,0:T(8,128)} pad(f32[7,2048]{1,0:T(8,128)} %param.7, f32[]{:T(128)} %constant.2.clone.1), padding=0_1x0_0 | pad | bytes 122884 | tf_op jit(solution)/shard_map/jit(_pad)/pad | solution.py:184
  2.1 114.8 %total.1 = (f32[8,256]{1,0:T(8,128)}, f32[32,8,2048]{2,1,0:T(8,128)}) custom-call(f32[8,2048]{1,0:T(8,128)} %pad.4.star_ref, s32[1,256]{1,0:T(1,128)} %bitcast.3), custom_call_target="tpu_custom_call" | custom-call | tf_op jit(solution)/shard_map/total/pallas_call | solution.py:187
  117.0 15.7 %finish.1 = (f32[6,256]{1,0:T(8,128)}, f32[12,256]{1,0:T(8,128)}) custom-call(s32[256]{0:T(256)} %bitcast.5, f32[32,8,2048]{2,1,0:T(8,128)} %get-tuple-element.4.every_ref, f32[8,2048]{1,0:T(8,128)} %pad.4.star_ref, s32[1,256]{1,0:T(1,128)} %bitcast.4, s32[256,128]{1,0:T(8,128)} %near_ref.1, f32[8,256]{1,0:T(8,128)} %get-tuple-element.5.total_ref, ...), custom_call_target="tpu_custom_call" | custom-call | tf_op jit(solution)/shard_map/finish/pallas_call | solution.py:202

commit v2 on v1

--- a/solution.py
+++ b/solution.py
@@ -9,6 +9,7 @@
 
 soft_sq = 0.01
 LANES = 128
+TILE = 256
 MESH = pl.DeviceIdType.MESH
 
 
@@ -65,14 +66,28 @@
     return jnp.transpose(wide)[:8, :]
 
 
-def total_kernel(axes, group, star_ref, index_ref, total_ref, slots, q_ref, acc_ref,
-                 send_sem, recv_sem, own_sem):
+def split3(x):
+    hi = x.astype(jnp.bfloat16).astype(jnp.float32)
+    rest = x - hi
+    mid = rest.astype(jnp.bfloat16).astype(jnp.float32)
+    low = (rest - mid).astype(jnp.bfloat16).astype(jnp.float32)
+    return hi, mid, low
+
+
+def split2(x):
+    hi = x.astype(jnp.bfloat16)
+    return hi, (x - hi.astype(jnp.float32)).astype(jnp.bfloat16)
+
+
+def total_kernel(axes, group, star_ref, index_ref, total_ref, slots, q_ref, qt_ref, qs_ref, star_parts,
+                 act_parts, acc_ref, send_sem, recv_sem, own_sem):
     rows, cols = axes
     n = rows * cols
     me = lax.axis_index("row") * cols + lax.axis_index("col")
     actives = index_ref.shape[1]
-    tiles = star_ref.shape[1] // LANES
+    stars = star_ref.shape[1]
     barrier = pltpu.get_barrier_semaphore()
+    f32 = jnp.float32
 
     def place(k):
         other = lax.rem(me + k, n)
@@ -84,22 +99,66 @@
 
     own = pltpu.make_async_copy(star_ref, slots.at[me], own_sem)
     own.start()
-    fill_states(star_ref, index_ref, q_ref)
+    for part in range(actives // LANES):
+        at = slice(part * LANES, (part + 1) * LANES)
+        idx = jnp.broadcast_to(index_ref[:, at], (8, LANES))
+        state = lane_gather(lambda t: star_ref[:, t * LANES : (t + 1) * LANES], stars // LANES, idx)
+        qs_ref[:, at] = state
+        turned = jnp.transpose(state)
+        qt_ref[at, 0:8] = turned
+        for c in range(3):
+            q_ref[c, at, :] = jnp.broadcast_to(turned[:, c : c + 1], (LANES, TILE))
     acc_ref[...] = jnp.zeros_like(acc_ref)
 
     def add_block(block):
-        @pl.loop(0, actives // (8 * group))
+        center = block[:, 0:1]
+        line = lax.broadcasted_iota(jnp.int32, (8, 1), 0)
+        here = block[...] - center
+        dots = jnp.sum(here[0:3] * here[3:6], axis=0, keepdims=True)
+        here = jnp.where(line == 6, 1.0, jnp.where(line == 7, dots, here))
+        hi, mid, low = split3(here)
+        zero = jnp.zeros_like(hi)
+        star_parts[...] = jnp.concatenate([hi, mid, low, hi, mid, hi, zero, zero], axis=0).astype(jnp.bfloat16)
+        mine = qs_ref[...] - center
+        both = jnp.sum(mine[0:3] * mine[3:6], axis=0, keepdims=True)
+        side = jnp.concatenate([-mine[3:6], -mine[0:3], both, jnp.ones_like(both)], axis=0)
+        hi, mid, low = split3(side)
+        zero = jnp.zeros_like(hi)
+        tall = jnp.concatenate([hi, hi, hi, mid, mid, low] + [zero] * 10, axis=0)
+        act_parts[...] = jnp.transpose(tall)[:, :64].astype(jnp.bfloat16)
+        shift = jnp.transpose(jnp.broadcast_to(center, (8, LANES)))[0:1, :]
+
+        @pl.loop(0, actives // group)
         def _(g):
-            for sub in range(group):
-                at = pl.ds(pl.multiple_of(g * (8 * group) + 8 * sub, 8), 8)
-                q = [q_ref[c, at, :] for c in range(6)]
-                acc = [acc_ref[c, at, :] for c in range(9)]
-                for t in range(tiles):
-                    lanes = slice(t * LANES, (t + 1) * LANES)
-                    star = [jnp.broadcast_to(block[c : c + 1, lanes], (8, LANES)) for c in range(7)]
-                    acc = pair_sums(q, star, acc)
-                for c in range(9):
-                    acc_ref[c, at, :] = acc[c]
+            at = pl.ds(pl.multiple_of(g * group, group), group)
+            parts = [[], [], [], []]
+            for t in range(stars // TILE):
+                lanes = slice(t * TILE, (t + 1) * TILE)
+                dv = jnp.dot(act_parts[at, :], star_parts[:, lanes], preferred_element_type=f32)
+                pieces = [[], [], [], []]
+                for sub in range(group // 16):
+                    ra = pl.ds(pl.multiple_of(g * group + 16 * sub, 16), 16)
+                    dx, dy, dz = [block[c : c + 1, lanes] - q_ref[c, ra, :] for c in range(3)]
+                    s = dx * dx + dy * dy + dz * dz + soft_sq
+                    r = lax.rsqrt(s)
+                    inv = r * r
+                    w = (block[6:7, lanes] * r) * inv
+                    wk = w * (dv[16 * sub : 16 * sub + 16] * inv)
+                    for i, p in enumerate(split2(w) + split2(wk)):
+                        pieces[i].append(p)
+                for i in range(4):
+                    parts[i].append(jnp.concatenate(pieces[i], axis=0))
+            full = [jnp.concatenate(p, axis=1) for p in parts]
+            table = star_parts[0:32, :]
+
+            def weigh(m):
+                return lax.dot_general(m, table, (((1,), (1,)), ((), ())), preferred_element_type=f32)
+
+            q = qt_ref[at, 0:8] - shift
+            for i in range(2):
+                out = weigh(full[2 * i]) + weigh(full[2 * i + 1])
+                out = out[:, 0:8] + out[:, 8:16] + out[:, 16:24]
+                acc_ref[i, at, :] += out - q * out[:, 6:7]
 
     def copy(k):
         return pltpu.make_async_remote_copy(
@@ -113,24 +172,27 @@
     def _(k):
         copy(k).start()
 
-    add_block(star_ref)
+    own.wait()
+
+    @pl.loop(0, n)
+    def _(k):
+        source = lax.rem(me + n - k, n)
+
+        @pl.when(k > 0)
+        def _():
+            pltpu.make_async_remote_copy(
+                src_ref=star_ref, dst_ref=slots.at[source], send_sem=send_sem.at[k],
+                recv_sem=recv_sem.at[k], device_id=place(k), device_id_type=MESH,
+            ).wait_recv()
+
+        add_block(slots.at[source])
 
     @pl.loop(1, n)
     def _(k):
-        source = lax.rem(me + n - k, n)
-        pltpu.make_async_remote_copy(
-            src_ref=star_ref, dst_ref=slots.at[source], send_sem=send_sem.at[k],
-            recv_sem=recv_sem.at[k], device_id=place(k), device_id_type=MESH,
-        ).wait_recv()
-        add_block(slots.at[source])
-
-    @pl.loop(1, n)
-    def _(k):
         copy(k).wait_send()
 
-    own.wait()
-    sums = [jnp.sum(acc_ref[c], axis=1, keepdims=True) for c in range(9)]
-    jerk = [sums[3 + c] - 3.0 * sums[6 + c] for c in range(3)]
+    sums = [acc_ref[0, :, c : c + 1] for c in range(6)]
+    jerk = [sums[3 + c] - 3.0 * acc_ref[1, :, c : c + 1] for c in range(3)]
     total_ref[...] = rows_of(sums[:3] + jerk)
 
 
@@ -190,8 +252,12 @@
         in_specs=[vmem, vmem],
         out_specs=(vmem, vmem),
         scratch_shapes=[
-            pltpu.VMEM((6, actives, LANES), f32),
-            pltpu.VMEM((9, actives, LANES), f32),
+            pltpu.VMEM((3, actives, TILE), f32),
+            pltpu.VMEM((actives, 8), f32),
+            pltpu.VMEM((8, actives), f32),
+            pltpu.VMEM((64, stars), jnp.bfloat16),
+            pltpu.VMEM((actives, 64), jnp.bfloat16),
+            pltpu.VMEM((2, actives, 8), f32),
             pltpu.SemaphoreType.DMA((n,)),
             pltpu.SemaphoreType.DMA((n,)),
             pltpu.SemaphoreType.DMA,
@@ -214,7 +280,7 @@
       step_size.reshape(1, actives))
 
 
-GROUP = 4
+GROUP = 64
 
 
 def solution(mesh):

time: 133 us -> 143 us (1.075)
  Pallas kernels: 131 us -> 140 us
    pallas_call x1, Pallas kernels: 115 us -> 125 us  [body(): pl.pallas_call(functools.partial(total_kernel, axes, GROUP), out_shape=(j...]
where the time goes in v2:
time: 143 us; the launch traced here: 142 us
  Pallas kernels  140 us (98%)
  local copies, waits for them, and re-layouts  1.48 us (1%)
    pallas_call x1, Pallas kernels, body(): pl.pallas_call(functools.partial(total_kernel, axes, GROUP), out_shape=(j...  125 us
    pallas_call x1, Pallas kernels, body(): pl.pallas_call(finish_kernel, out_shape=(jax.ShapeDtypeStruct((6, actives...  15.7 us

profile of v2, /device:TPU:25, one launch (start us, length us, event | category | flops | bytes accessed | tf_op | source)
XLA Modules:
  0.0 142.3 jit_solution(10402450891571799015)
XLA Ops:
  0.6 1.5 %pad.4.star_ref = f32[8,2048]{1,0:T(8,128)} pad(f32[7,2048]{1,0:T(8,128)} %param.7, f32[]{:T(128)} %constant.2.clone.1), padding=0_1x0_0 | pad | bytes 122884 | tf_op jit(solution)/shard_map/jit(_pad)/pad | solution.py:246
  2.1 124.5 %total.1 = (f32[8,256]{1,0:T(8,128)}, f32[32,8,2048]{2,1,0:T(8,128)}) custom-call(f32[8,2048]{1,0:T(8,128)} %pad.4.star_ref, s32[1,256]{1,0:T(1,128)} %bitcast.3), custom_call_target="tpu_custom_call" | custom-call | tf_op jit(solution)/shard_map/total/pallas_call | solution.py:249
  126.6 15.7 %finish.1 = (f32[6,256]{1,0:T(8,128)}, f32[12,256]{1,0:T(8,128)}) custom-call(s32[256]{0:T(256)} %bitcast.5, f32[32,8,2048]{2,1,0:T(8,128)} %get-tuple-element.4.every_ref, f32[8,2048]{1,0:T(8,128)} %pad.4.star_ref, s32[1,256]{1,0:T(1,128)} %bitcast.4, s32[256,128]{1,0:T(8,128)} %near_ref.1, f32[8,256]{1,0:T(8,128)} %get-tuple-element.5.total_ref, ...), custom_call_target="tpu_custom_call" | custom-call | tf_op jit(solution)/shard_map/finish/pallas_call | solution.py:268

commit v3 on v2

--- a/solution.py
+++ b/solution.py
@@ -9,6 +9,7 @@
 
 soft_sq = 0.01
 LANES = 128
+WIDE = 4
 TILE = 256
 MESH = pl.DeviceIdType.MESH
 
@@ -79,7 +80,7 @@
     return hi, (x - hi.astype(jnp.float32)).astype(jnp.bfloat16)
 
 
-def total_kernel(axes, group, star_ref, index_ref, total_ref, slots, q_ref, qt_ref, qs_ref, star_parts,
+def total_kernel(axes, group, star_ref, index_ref, total_ref, slots, q_ref, qt_ref, qs_ref, star_parts, sum_parts,
                  act_parts, acc_ref, send_sem, recv_sem, own_sem):
     rows, cols = axes
     n = rows * cols
@@ -119,6 +120,8 @@
         hi, mid, low = split3(here)
         zero = jnp.zeros_like(hi)
         star_parts[...] = jnp.concatenate([hi, mid, low, hi, mid, hi, zero, zero], axis=0).astype(jnp.bfloat16)
+        heavy = split3(here * block[6:7, :])
+        sum_parts[...] = jnp.concatenate(list(heavy) + [zero], axis=0).astype(jnp.bfloat16)
         mine = qs_ref[...] - center
         both = jnp.sum(mine[0:3] * mine[3:6], axis=0, keepdims=True)
         side = jnp.concatenate([-mine[3:6], -mine[0:3], both, jnp.ones_like(both)], axis=0)
@@ -142,23 +145,24 @@
                     s = dx * dx + dy * dy + dz * dz + soft_sq
                     r = lax.rsqrt(s)
                     inv = r * r
-                    w = (block[6:7, lanes] * r) * inv
+                    w = r * inv
                     wk = w * (dv[16 * sub : 16 * sub + 16] * inv)
                     for i, p in enumerate(split2(w) + split2(wk)):
                         pieces[i].append(p)
                 for i in range(4):
                     parts[i].append(jnp.concatenate(pieces[i], axis=0))
             full = [jnp.concatenate(p, axis=1) for p in parts]
-            table = star_parts[0:32, :]
+            table = sum_parts[...]
 
             def weigh(m):
                 return lax.dot_general(m, table, (((1,), (1,)), ((), ())), preferred_element_type=f32)
 
             q = qt_ref[at, 0:8] - shift
+            out = weigh(jnp.concatenate(full, axis=0))
+            out = out[:, 0:8] + out[:, 8:16] + out[:, 16:24]
             for i in range(2):
-                out = weigh(full[2 * i]) + weigh(full[2 * i + 1])
-                out = out[:, 0:8] + out[:, 8:16] + out[:, 16:24]
-                acc_ref[i, at, :] += out - q * out[:, 6:7]
+                got = out[2 * i * group : (2 * i + 1) * group] + out[(2 * i + 1) * group : (2 * i + 2) * group]
+                acc_ref[i, at, :] += got - q * got[:, 6:7]
 
     def copy(k):
         return pltpu.make_async_remote_copy(
@@ -202,26 +206,27 @@
     tiles = star_ref.shape[1] // LANES
     fill_states(star_ref, index_ref, q_ref)
 
-    @pl.loop(0, actives // 8)
+    @pl.loop(0, actives // (8 * WIDE))
     def _(g):
-        base = pl.multiple_of(g * 8, 8)
-        near = near_ref[pl.ds(base, 8), :]
-        for i in range(8):
-            block = every_ref.at[target_ref[base + i]]
-            idx = jnp.broadcast_to(near[i : i + 1, :], (8, LANES))
-            tile_ref[pl.ds(8 * i, 8), :] = lane_gather(
-                lambda t: block[:, t * LANES : (t + 1) * LANES], tiles, idx
-            )
-        star = [tile_ref[pl.ds(c, 8, stride=8), :] for c in range(7)]
-        q = [q_ref[c, pl.ds(base, 8), :] for c in range(6)]
-        acc = pair_sums(q, star, [jnp.zeros((8, LANES), jnp.float32)] * 9)
         lane = lax.broadcasted_iota(jnp.int32, (8, LANES), 1)
-        wide = jnp.zeros((8, LANES), jnp.float32)
-        for c in range(3):
-            wide = jnp.where(lane == c, jnp.sum(acc[c], axis=1, keepdims=True), wide)
-            jerk = jnp.sum(acc[3 + c] - 3.0 * acc[6 + c], axis=1, keepdims=True)
-            wide = jnp.where(lane == 3 + c, jerk, wide)
-        irr_ref[pl.ds(base, 8), :] = wide
+        for part in range(WIDE):
+            base = pl.multiple_of((g * WIDE + part) * 8, 8)
+            near = near_ref[pl.ds(base, 8), :]
+            for i in range(8):
+                block = every_ref.at[target_ref[base + i]]
+                idx = jnp.broadcast_to(near[i : i + 1, :], (8, LANES))
+                tile_ref[pl.ds(64 * part + 8 * i, 8), :] = lane_gather(
+                    lambda t: block[:, t * LANES : (t + 1) * LANES], tiles, idx
+                )
+            star = [tile_ref[pl.ds(64 * part + c, 8, stride=8), :] for c in range(7)]
+            q = [q_ref[c, pl.ds(base, 8), :] for c in range(6)]
+            acc = pair_sums(q, star, [jnp.zeros((8, LANES), jnp.float32)] * 9)
+            wide = jnp.zeros((8, LANES), jnp.float32)
+            for c in range(3):
+                wide = jnp.where(lane == c, jnp.sum(acc[c], axis=1, keepdims=True), wide)
+                jerk = jnp.sum(acc[3 + c] - 3.0 * acc[6 + c], axis=1, keepdims=True)
+                wide = jnp.where(lane == 3 + c, jerk, wide)
+            irr_ref[pl.ds(base, 8), :] = wide
 
     irregular = jnp.transpose(irr_ref[...])[:6, :]
     total = total_ref[:6, :]
@@ -247,7 +252,7 @@
     index = active_index.reshape(1, actives)
     f32 = jnp.float32
     total, every = pl.pallas_call(
-        functools.partial(total_kernel, axes, GROUP),
+        functools.partial(total_kernel, axes, actives),
         out_shape=(jax.ShapeDtypeStruct((8, actives), f32), jax.ShapeDtypeStruct((n, 8, stars), f32)),
         in_specs=[vmem, vmem],
         out_specs=(vmem, vmem),
@@ -256,6 +261,7 @@
             pltpu.VMEM((actives, 8), f32),
             pltpu.VMEM((8, actives), f32),
             pltpu.VMEM((64, stars), jnp.bfloat16),
+            pltpu.VMEM((32, stars), jnp.bfloat16),
             pltpu.VMEM((actives, 64), jnp.bfloat16),
             pltpu.VMEM((2, actives, 8), f32),
             pltpu.SemaphoreType.DMA((n,)),
@@ -272,15 +278,12 @@
         out_specs=(vmem, vmem),
         scratch_shapes=[
             pltpu.VMEM((6, actives, LANES), f32),
-            pltpu.VMEM((64, LANES), f32),
+            pltpu.VMEM((64 * WIDE, LANES), f32),
             pltpu.VMEM((actives, LANES), f32),
         ],
         name="finish",
     )(assignment[:, 0], every, star8, index, neighbour_index, total, start_state, old_derivs,
       step_size.reshape(1, actives))
-
-
-GROUP = 64
 
 
 def solution(mesh):

time: 143 us -> 113 us (0.79)
  Pallas kernels: 140 us -> 111 us
    pallas_call x1, Pallas kernels: 125 us -> 98.4 us  [body(): pl.pallas_call(functools.partial(total_kernel, axes, actives), out_shape=...]
    pallas_call x1, Pallas kernels: 15.7 us -> 12.6 us  [body(): pl.pallas_call(finish_kernel, out_shape=(jax.ShapeDtypeStruct((6, actives...]
where the time goes in v3:
time: 113 us
  Pallas kernels  111 us (98%)
  local copies, waits for them, and re-layouts  1.48 us (1%)
    pallas_call x1, Pallas kernels, body(): pl.pallas_call(functools.partial(total_kernel, axes, actives), out_shape=...  98.4 us
    pallas_call x1, Pallas kernels, body(): pl.pallas_call(finish_kernel, out_shape=(jax.ShapeDtypeStruct((6, actives...  12.6 us

profile of v3, /device:TPU:25, one launch (start us, length us, event | category | flops | bytes accessed | tf_op | source)
XLA Modules:
  0.0 113.2 jit_solution(3976364875804764575)
XLA Ops:
  0.6 1.5 %pad.4.star_ref = f32[8,2048]{1,0:T(8,128)} pad(f32[7,2048]{1,0:T(8,128)} %param.7, f32[]{:T(128)} %constant.2.clone.1), padding=0_1x0_0 | pad | bytes 122884 | tf_op jit(solution)/shard_map/jit(_pad)/pad | solution.py:251
  2.1 98.4 %total.1 = (f32[8,256]{1,0:T(8,128)}, f32[32,8,2048]{2,1,0:T(8,128)}) custom-call(f32[8,2048]{1,0:T(8,128)} %pad.4.star_ref, s32[1,256]{1,0:T(1,128)} %bitcast.3), custom_call_target="tpu_custom_call" | custom-call | tf_op jit(solution)/shard_map/total/pallas_call | solution.py:254
  100.5 12.6 %finish.1 = (f32[6,256]{1,0:T(8,128)}, f32[12,256]{1,0:T(8,128)}) custom-call(s32[256]{0:T(256)} %bitcast.5, f32[32,8,2048]{2,1,0:T(8,128)} %get-tuple-element.4.every_ref, f32[8,2048]{1,0:T(8,128)} %pad.4.star_ref, s32[1,256]{1,0:T(1,128)} %bitcast.4, s32[256,128]{1,0:T(8,128)} %near_ref.1, f32[8,256]{1,0:T(8,128)} %get-tuple-element.5.total_ref, ...), custom_call_target="tpu_custom_call" | custom-call | tf_op jit(solution)/shard_map/finish/pallas_call | solution.py:274
